TPU v7x, 32 devices: a whole 2x2x4 slice. The times are simulated.
32 devices in a mesh: row: 8 (over y, x, core), col: 4 (over z).
Axes of the slice: x: 2, y: 2, z: 4, core: 2. Of those that a mesh axis runs over, the one named last changes fastest.
Arguments:
- in_map: bfloat16 [128, 128, 256], P('row', 'col'), may hold values from -6 to 6
- tile_w: bfloat16 [3, 3, 256, 256], replicated, may hold values from -0.125 to 0.125
- head_w1: bfloat16 [3, 3, 256, 256], replicated, may hold values from -0.125 to 0.125
- head_w2: bfloat16 [3, 3, 256, 256], replicated, may hold values from -0.125 to 0.125
- box_row: int32 [64, 4], P('row', 'col'), may hold values from 0 to 2
- box_col: int32 [64, 4], P('row', 'col'), may hold values from 0 to 18
- box_target: int32 [64, 4], P('row', 'col'), may hold values from -1 to 15, as said below
- head_cot: bfloat16 [32, 4, 14, 14, 256], P('row', 'col'), may hold values from -6 to 6
Outputs:
- grad_map: bfloat16 [128, 128, 256], P('row', 'col')
- grad_w1: float32 [3, 3, 256, 256], replicated
- grad_w2: float32 [3, 3, 256, 256], replicated
Inputs may be any that keep to these rules, and one draw needn't show every extreme that they name: `box_target`: within each row r of tiles, every head slot d * 4 + h (d below 4, h below 4) is named by exactly one tile slot, and empty slots hold -1. A tile names at most 2 head slots of one device, so it holds at most 8 boxes; in every row of tiles one tile holds 8 boxes, 2 for each device of the row.
All inputs are finite; a program needn't handle non-finite values.
Results may differ from a plain program's by a relative error of at most 0.012.
Values may be sent and summed in bfloat16 or wider, within the bound.
No kernel may reach another device: no remote copies, remote signals or barrier semaphores. Data moves between devices by JAX's collectives and lax.ppermute only.
A program may use at most 64 MiB of HBM per device.

v0:
```python
import math
import jax
import jax.numpy as jnp
from jax import lax
from jax.sharding import PartitionSpec as P

LAYOUT = ("NHWC", "HWIO", "NHWC")


def padded_2(shard, sides, width):
    for axis, dim in sides:
        size, length = (lax.axis_size(axis), shard.shape[dim])
        up = [(i, (i + 1) % size) for i in range(size - 1)]
        down = [(j, i) for i, j in up]
        last = lax.slice_in_dim(shard, length - width, length, axis=dim)
        leading = lax.slice_in_dim(shard, 0, width, axis=dim)
        before = lax.ppermute(last, axis, up)
        after = lax.ppermute(leading, axis, down)
        shard = jnp.concatenate([before, shard, after], axis=dim)
    return shard


def conv_pad(inputs, kernel, margin):
    return lax.conv_general_dilated(
        inputs,
        kernel,
        (1, 1),
        ((margin, margin), (margin, margin)),
        dimension_numbers=LAYOUT,
        preferred_element_type=jnp.float32,
    )


def flip_weights(kernel):
    return jnp.transpose(jnp.flip(kernel, (0, 1)), (0, 1, 3, 2))


def silu_slope(values):
    sigma = jax.nn.sigmoid(values)
    return sigma * (1.0 + values * (1.0 - sigma))


def weight_grad(inputs, deltas):
    channels = inputs.shape[-1]
    box_side = inputs.shape[1]
    padded = jnp.pad(inputs, ((0, 0), (1, 1), (1, 1), (0, 0)))
    flat_delta = deltas.reshape(-1, channels)
    blocks = []
    for shift_y in range(3):
        for shift_x in range(3):
            window = padded[
                :, shift_y : shift_y + box_side, shift_x : shift_x + box_side, :
            ].reshape(-1, channels)
            blocks.append(
                lax.dot_general(
                    window, flat_delta, (((0,), (0,)), ((), ())), preferred_element_type=jnp.float32
                )
            )
    return jnp.stack(blocks).reshape(3, 3, channels, channels)


def pick_rows(table, values):
    flat = values.reshape(values.shape[0], -1)
    return jnp.dot(table, flat, preferred_element_type=jnp.float32).astype(jnp.bfloat16)


def pick_back(table, values):
    return lax.dot_general(
        table, values, (((0,), (0,)), ((), ())), preferred_element_type=jnp.float32
    ).astype(jnp.bfloat16)


def body(in_map, tile_w, head_w1, head_w2, box_row, box_col, box_target, head_cot):
    tile_rows, tile_cols, channels = in_map.shape
    head_count = head_cot.shape[0]
    box_side = head_cot.shape[2]
    slot_count = box_target.shape[0]
    columns = lax.axis_size("col")
    capacity = slot_count // columns
    pair_count = columns * capacity
    padded = padded_2(in_map, (("row", 0), ("col", 1)), 1)
    preact = conv_pad(padded[None], tile_w, 0)[0]
    target = box_target[:, 0]
    occupied = target >= 0
    dest_col = jnp.where(occupied, target // head_count, 0)
    head_slot = jnp.where(occupied, target % head_count, 0)
    slot_ids = jnp.arange(slot_count, dtype=jnp.int32)
    same_dest = (dest_col[:, None] == dest_col[None, :]) & occupied[None, :]
    placing = jnp.sum(same_dest & (slot_ids[None, :] < slot_ids[:, None]), axis=1)
    pair_slot = dest_col * capacity + placing
    pair_ids = jnp.arange(pair_count, dtype=jnp.int32)
    send_map = ((pair_slot[None, :] == pair_ids[:, None]) & occupied[None, :]).astype(jnp.bfloat16)
    head_ids = jnp.arange(head_count, dtype=jnp.int32)
    head_hot = ((head_slot[:, None] == head_ids[None, :]) & occupied[:, None]).astype(jnp.bfloat16)
    pair_head = (
        jnp.dot(send_map, head_hot, preferred_element_type=jnp.float32)
        .astype(jnp.bfloat16)
        .reshape(columns, capacity, head_count)
    )
    top_row = box_row[:, 0]
    left_col = box_col[:, 0]
    zero_index = jnp.zeros((), jnp.int32)
    window = box_side + 2
    windows = jax.vmap(
        lambda y, x: lax.dynamic_slice(padded, (y, x, zero_index), (window, window, channels))
    )(top_row, left_col)
    outgoing = pick_rows(send_map, windows).reshape(columns, capacity, window, window, channels)
    arrived, arrived_head = (
        lax.all_to_all(outgoing, "col", split_axis=0, concat_axis=0, tiled=True),
        lax.all_to_all(pair_head, "col", split_axis=0, concat_axis=0, tiled=True),
    )
    arrived_head = arrived_head.reshape(pair_count, head_count)
    gathered = pick_back(arrived_head, arrived.reshape(pair_count, -1)).reshape(
        head_count, window, window, channels
    )
    box_input = jax.nn.silu(conv_pad(gathered, tile_w, 0)).astype(jnp.bfloat16)
    factor = 1.0 / math.sqrt(lax.axis_size("row") * columns * head_count * box_side * box_side)
    cotangent = head_cot[:, 0]
    pre_one = conv_pad(box_input, head_w1, 1)
    hidden = jax.nn.silu(pre_one).astype(jnp.bfloat16)
    pre_two = conv_pad(hidden, head_w2, 1)
    delta_two = (cotangent.astype(jnp.float32) * silu_slope(pre_two)).astype(jnp.bfloat16)
    second_local = weight_grad(hidden, delta_two)
    delta_one = (conv_pad(delta_two, flip_weights(head_w2), 1) * silu_slope(pre_one)).astype(
        jnp.bfloat16
    )
    box_grads = conv_pad(delta_one, flip_weights(head_w1), 1).astype(jnp.bfloat16)
    sent_back = pick_rows(arrived_head, box_grads).reshape(
        columns, capacity, box_side, box_side, channels
    )
    returned = lax.all_to_all(sent_back, "col", split_axis=0, concat_axis=0, tiled=True)
    slot_grads = pick_back(send_map, returned.reshape(pair_count, -1)).reshape(
        slot_count, box_side, box_side, channels
    )
    first_local = weight_grad(box_input, delta_one)
    first_sum, second_sum = lax.psum((first_local, second_local), ("row", "col"))

    def add_box(slot, running):
        current = lax.dynamic_slice(
            running, (top_row[slot], left_col[slot], zero_index), (box_side, box_side, channels)
        )
        return lax.dynamic_update_slice(
            running,
            current + slot_grads[slot].astype(jnp.float32),
            (top_row[slot], left_col[slot], zero_index),
        )

    box_total = lax.fori_loop(
        0, slot_count, add_box, jnp.zeros((tile_rows, tile_cols, channels), jnp.float32)
    )
    delta_map = (box_total * silu_slope(preact)).astype(jnp.bfloat16)
    delta_rim = padded_2(delta_map, (("row", 0), ("col", 1)), 1)
    grad_map = conv_pad(delta_rim[None], flip_weights(tile_w), 0)[0].astype(jnp.bfloat16)
    return (grad_map, first_sum * factor, second_sum * factor)


def solution(mesh):
    in_specs = (
        P("row", "col", None),
        P(),
        P(),
        P(),
        P("row", "col"),
        P("row", "col"),
        P("row", "col"),
        P("row", "col", None, None, None),
    )
    out_specs = (P("row", "col", None), P(), P())
    return jax.shard_map(body, mesh=mesh, in_specs=in_specs, out_specs=out_specs, check_vma=False)
```

profile of v0, /device:TPU:0, one launch (start us, length us, event | category | flops | bytes accessed | tf_op | source)
XLA Modules:
  0.0 296.8 jit_solution(2329614647910186350)
XLA Ops:
  8.0 1.3 collective-permute-start.1
  9.3 3.0 %collective-permute-start = (bf16[1,32,256]{2,1,0:T(8,128)(2,1)S(1)}, bf16[1,32,256]{2,1,0:T(8,128)(2,1)S(1)}, u32[]{:S(2)}, u32[]{:S(2)}) collective-permute-start(bf16[1,32,256]{2,1,0:T(8,128)(2,1)S(1)} %get-tuple-element.174), channel_id=1, source_target_pairs={{0,4},{4,8},{8,12},{12,16},{16,20},{20,24},{24,28},{1,5},{5,9},{9,... | collective-permute-start | bytes 49160 | tf_op jit(solution)/shard_map/ppermute | solution.py:17
  16.9 5.0 %collective-permute-start.2 = (bf16[18,1,256]{2,1,0:T(2,128)(2,1)S(1)}, bf16[18,1,256]{2,1,0:T(2,128)(2,1)S(1)}, u32[]{:S(2)}, u32[]{:S(2)}) collective-permute-start(bf16[18,1,256]{2,1,0:T(2,128)(2,1)S(1)} %get-tuple-element.169), channel_id=1, source_target_pairs={{0,1},{1,2},{2,3},{4,5},{5,6},{6,7},{8,9},{9,10},{10,11},{12,13},{... | collective-permute-start | bytes 27656 | tf_op jit(solution)/shard_map/ppermute | solution.py:17
  21.9 1.3 collective-permute-start.3
  23.3 4.3 %collective-permute-done.3 = bf16[18,1,256]{2,1,0:T(2,128)(2,1)S(1)} collective-permute-done((bf16[18,1,256]{2,1,0:T(2,128)(2,1)S(1)}, bf16[18,1,256]{2,1,0:T(2,128)(2,1)S(1)}, u32[]{:S(2)}, u32[]{:S(2)}) %collective-permute-start.3) | collective-permute-done | bytes 9248 | tf_op jit(solution)/shard_map/ppermute | solution.py:18
  27.8 20.0 %while.15 = (s32[]{:T(128)}, bf16[18,34,256]{2,1,0:T(8,128)(2,1)S(1)}, s32[8,3]{0,1:T(4,128)S(1)}, bf16[8,16,16,256]{3,2,1,0:T(8,128)(2,1)}, s32[]{:T(128)}) while((s32[]{:T(128)}, bf16[18,34,256]{2,1,0:T(8,128)(2,1)S(1)}, s32[8,3]{0,1:T(4,128)S(1)}, bf16[8,16,16,256]{3,2,1,0:T(8,128)(2,1)}, s32[]{:T(128)}) %tuple.64), condition=%wide.while_cond, body=%wide.while_body.sunk | while | flops 2 | bytes 263285 | solution.py:105
  28.4 1.9 bitcast_dynamic-update-slice_fusion.2
  30.9 1.9 bitcast_dynamic-update-slice_fusion.2
  33.4 1.9 bitcast_dynamic-update-slice_fusion.2
  35.9 1.9 bitcast_dynamic-update-slice_fusion.2
  38.4 1.9 bitcast_dynamic-update-slice_fusion.2
  40.9 1.9 bitcast_dynamic-update-slice_fusion.2
  43.4 1.9 bitcast_dynamic-update-slice_fusion.2
  45.9 1.9 bitcast_dynamic-update-slice_fusion.2
  47.8 1.8 copy.157
  50.0 1.2 copy.158
  51.2 4.0 %all-to-all-start.1 = ((bf16[4,2,16,16,256]{4,3,2,1,0:T(8,128)(2,1)}), bf16[4,2,16,16,256]{4,3,2,1,0:T(8,128)(2,1)S(1)}, u32[]{:S(2)}, u32[]{:S(2)}) async-start(bf16[4,2,16,16,256]{4,3,2,1,0:T(8,128)(2,1)} %bitcast.140), calls=%async_computation.1 | async-start | bytes 2097152 | tf_op jit(solution)/shard_map/all_to_all | solution.py:109
  57.3 1.1 copy.111
  58.4 22.7 %all-to-all-done.1 = bf16[4,2,16,16,256]{4,3,2,1,0:T(8,128)(2,1)S(1)} async-done(((bf16[4,2,16,16,256]{4,3,2,1,0:T(8,128)(2,1)}), bf16[4,2,16,16,256]{4,3,2,1,0:T(8,128)(2,1)S(1)}, u32[]{:S(2)}, u32[]{:S(2)}) %all-to-all-start.1) | async-done | bytes 1048608 | tf_op jit(solution)/shard_map/all_to_all | solution.py:109
  81.0 3.4 %all-to-all-start = ((bf16[4,2,4]{2,1,0:T(2,128)(2,1)}), bf16[4,2,4]{2,1,0:T(2,128)(2,1)S(1)}, u32[]{:S(2)}, u32[]{:S(2)}) async-start(bf16[4,2,4]{2,1,0:T(2,128)(2,1)} %bitcast.9), calls=%async_computation | async-start | bytes 4096 | tf_op jit(solution)/shard_map/all_to_all | solution.py:110
  84.9 4.8 %all-to-all-done = bf16[4,2,4]{2,1,0:T(2,128)(2,1)S(1)} async-done(((bf16[4,2,4]{2,1,0:T(2,128)(2,1)}), bf16[4,2,4]{2,1,0:T(2,128)(2,1)S(1)}, u32[]{:S(2)}, u32[]{:S(2)}) %all-to-all-start) | async-done | bytes 96 | tf_op jit(solution)/shard_map/all_to_all | solution.py:110
  90.9 1.3 multiply_convert_fusion.1
  93.4 1.2 fusion.43
  94.7 1.1 select_bitcast_fusion.1
  96.4 1.3 add_multiply_fusion
  99.1 1.2 fusion.62
  101.6 2.9 fusion.9
  106.2 2.3 copy.120
  108.4 1.2 reshape.164
  111.4 2.5 convolution_convert_fusion.4
  116.3 1.8 copy.105
  118.1 3.5 %all-to-all-start.2 = ((bf16[4,2,14,14,256]{4,1,3,2,0:T(2,128)(2,1)}), bf16[4,2,14,14,256]{4,1,3,2,0:T(2,128)(2,1)S(1)}, u32[]{:S(2)}, u32[]{:S(2)}) async-start(bf16[4,2,14,14,256]{4,1,3,2,0:T(2,128)(2,1)} %copy.105), calls=%async_computation.2 | async-start | bytes 1605632 | tf_op jit(solution)/shard_map/all_to_all | solution.py:131
  121.6 1.4 fusion.28
  130.5 1.1 fusion.17
  134.0 1.3 fusion.14
  136.5 1.1 fusion.12
  137.6 1.1 fusion.11
  138.6 1.8 all-to-all-done.2
  141.9 45.4 %while.14 = (s32[]{:T(128)}, f32[16,32,256]{2,0,1:T(8,128)S(1)}, s32[8]{0:T(128)S(1)}, s32[8]{0:T(128)S(1)}, bf16[8,14,14,256]{3,2,1,0:T(8,128)(2,1)S(1)}, /*index=5*/s32[]{:T(128)}, s32[]{:T(128)}, s32[]{:T(128)}, s32[]{:T(128)}) while((s32[]{:T(128)}, f32[16,32,256]{2,0,1:T(8,128)S(1)}, s32[8]{0:T(128)S(1)}, s32[8]{0:T(128)S(1)}, ...), condition=%wide.region_2.3_spmd, body=%wide.region_1.2_spmd.sunk | while | flops 100360 | bytes 1706193 | solution.py:148
  187.6 1.3 collective-permute-start.4
  188.9 1.3 collective-permute-start.5
  190.2 4.3 %collective-permute-done.5 = bf16[1,32,256]{2,0,1:T(2,128)(2,1)S(1)} collective-permute-done((bf16[1,32,256]{2,0,1:T(2,128)(2,1)S(1)}, bf16[1,32,256]{2,0,1:T(2,128)(2,1)S(1)}, u32[]{:S(2)}, u32[]{:S(2)}) %collective-permute-start.5) | collective-permute-done | bytes 16416 | tf_op jit(solution)/shard_map/ppermute | solution.py:18
  194.6 1.8 collective-permute-start.6
  196.4 1.3 collective-permute-start.7
  197.8 4.2 %collective-permute-done.7 = bf16[18,1,256]{2,0,1:T(8,128)(2,1)S(1)} collective-permute-done((bf16[18,1,256]{2,0,1:T(8,128)(2,1)S(1)}, bf16[18,1,256]{2,0,1:T(8,128)(2,1)S(1)}, u32[]{:S(2)}, u32[]{:S(2)}) %collective-permute-start.7) | collective-permute-done | bytes 9248 | tf_op jit(solution)/shard_map/ppermute | solution.py:18
  204.3 80.6 %all-reduce.5.cloned.1.call-done = (f32[3,3,256,256]{3,2,1,0:T(8,128)}, f32[3,3,256,256]{3,2,1,0:T(8,128)}) async-done(((f32[3,3,256,256]{3,2,1,0:T(8,128)}, f32[3,3,256,256]{3,2,1,0:T(8,128)}), (f32[3,3,256,256]{3,2,1,0:T(8,128)}, f32[3,3,256,256]{3,2,1,0:T(8,128)})) %all-reduce.5.cloned.1.call-update) | async-done | bytes 4718608 | tf_op jit(solution)/shard_map/psum | solution.py:136
  284.9 3.4 %broadcast_multiply_fusion.1 = f32[3,3,256,256]{3,2,1,0:T(8,128)} fusion(f32[3,3,256,256]{3,2,1,0:T(8,128)} %get-tuple-element.153), kind=kLoop, calls=%fused_computation.29 | loop fusion | flops 589824 | bytes 4718592 | tf_op jit(solution)/shard_map/mul | solution.py:154
  288.3 1.6 broadcast_multiply_fusion
  (196 shorter events, 53.8 us)
Async XLA Ops:
  7.2 49.2 %copy-start = (bf16[3,3,256,256]{3,2,1,0:T(8,128)(2,1)S(1)}, bf16[3,3,256,256]{3,2,1,0:T(8,128)(2,1)}, u32[]{:S(2)}) copy-start(bf16[3,3,256,256]{3,2,1,0:T(8,128)(2,1)} %param.11) | copy-start | bytes 3538948
  8.0 8.8 %collective-permute-start.1 = (bf16[1,32,256]{2,1,0:T(8,128)(2,1)S(1)}, bf16[1,32,256]{2,1,0:T(8,128)(2,1)S(1)}, u32[]{:S(2)}, u32[]{:S(2)}) collective-permute-start(bf16[1,32,256]{2,1,0:T(8,128)(2,1)S(1)} %get-tuple-element.173), channel_id=1, source_target_pairs={{4,0},{8,4},{12,8},{16,12},{20,16},{24,20},{28,24},{5,1},{9,5},{13... | collective-permute-start | bytes 49160 | tf_op jit(solution)/shard_map/ppermute | solution.py:18
  9.3 6.6 %collective-permute-start = (bf16[1,32,256]{2,1,0:T(8,128)(2,1)S(1)}, bf16[1,32,256]{2,1,0:T(8,128)(2,1)S(1)}, u32[]{:S(2)}, u32[]{:S(2)}) collective-permute-start(bf16[1,32,256]{2,1,0:T(8,128)(2,1)S(1)} %get-tuple-element.174), channel_id=1, source_target_pairs={{0,4},{4,8},{8,12},{12,16},{16,20},{20,24},{24,28},{1,5},{5,9},{9,... | collective-permute-start | bytes 49160 | tf_op jit(solution)/shard_map/ppermute | solution.py:17
  16.9 6.4 %collective-permute-start.2 = (bf16[18,1,256]{2,1,0:T(2,128)(2,1)S(1)}, bf16[18,1,256]{2,1,0:T(2,128)(2,1)S(1)}, u32[]{:S(2)}, u32[]{:S(2)}) collective-permute-start(bf16[18,1,256]{2,1,0:T(2,128)(2,1)S(1)} %get-tuple-element.169), channel_id=1, source_target_pairs={{0,1},{1,2},{2,3},{4,5},{5,6},{6,7},{8,9},{9,10},{10,11},{12,13},{... | collective-permute-start | bytes 27656 | tf_op jit(solution)/shard_map/ppermute | solution.py:17
  21.9 5.7 %collective-permute-start.3 = (bf16[18,1,256]{2,1,0:T(2,128)(2,1)S(1)}, bf16[18,1,256]{2,1,0:T(2,128)(2,1)S(1)}, u32[]{:S(2)}, u32[]{:S(2)}) collective-permute-start(bf16[18,1,256]{2,1,0:T(2,128)(2,1)S(1)} %get-tuple-element.170), channel_id=1, source_target_pairs={{1,0},{2,1},{3,2},{5,4},{6,5},{7,6},{9,8},{10,9},{11,10},{13,12},{... | collective-permute-start | bytes 27656 | tf_op jit(solution)/shard_map/ppermute | solution.py:18
  50.0 5.2 %copy-start.19 = (s32[8,1]{0,1:T(1,128)S(1)}, s32[8,1]{0,1:T(1,128)}, u32[]{:S(2)}) copy-start(s32[8,1]{0,1:T(1,128)} %param.16) | copy-start | bytes 100
  51.2 5.2 %copy-start.20 = (pred[8,5]{0,1:T(8,128)(4,1)S(1)}, pred[8,5]{0,1:T(8,128)(4,1)}, u32[]{:S(2)}) copy-start(pred[8,5]{0,1:T(8,128)(4,1)} %constant.129) | copy-start | bytes 124
  51.2 29.9 %all-to-all-start.1 = ((bf16[4,2,16,16,256]{4,3,2,1,0:T(8,128)(2,1)}), bf16[4,2,16,16,256]{4,3,2,1,0:T(8,128)(2,1)S(1)}, u32[]{:S(2)}, u32[]{:S(2)}) async-start(bf16[4,2,16,16,256]{4,3,2,1,0:T(8,128)(2,1)} %bitcast.140), calls=%async_computation.1 | async-start | bytes 2097152 | tf_op jit(solution)/shard_map/all_to_all | solution.py:109
  81.0 8.7 %all-to-all-start = ((bf16[4,2,4]{2,1,0:T(2,128)(2,1)}), bf16[4,2,4]{2,1,0:T(2,128)(2,1)S(1)}, u32[]{:S(2)}, u32[]{:S(2)}) async-start(bf16[4,2,4]{2,1,0:T(2,128)(2,1)} %bitcast.9), calls=%async_computation | async-start | bytes 4096 | tf_op jit(solution)/shard_map/all_to_all | solution.py:110
  90.2 0.7 copy-start.14
  92.2 1.3 copy-start.18
  94.7 1.2 copy-start.8
  94.7 1.8 copy-start.17
  100.3 0.8 copy-start.6
  105.3 6.1 %copy-start.4 = (bf16[14,4,16,256]{3,2,1,0:T(8,128)(2,1)}, bf16[14,4,16,256]{3,2,1,0:T(8,128)(2,1)S(1)}, u32[]{:S(2)}) copy-start(bf16[14,4,16,256]{3,2,1,0:T(8,128)(2,1)S(1)} %reshape.159) | copy-start | bytes 1376260
  116.3 5.3 %copy-start.10 = (bf16[4,14,14,256]{3,2,1,0:T(8,128)(2,1)S(1)}, bf16[4,14,14,256]{3,2,1,0:T(8,128)(2,1)}, u32[]{:S(2)}) copy-start(bf16[4,14,14,256]{3,2,1,0:T(8,128)(2,1)} %copy_bitcast_fusion.2) | copy-start | bytes 1204228
  118.1 22.3 %all-to-all-start.2 = ((bf16[4,2,14,14,256]{4,1,3,2,0:T(2,128)(2,1)}), bf16[4,2,14,14,256]{4,1,3,2,0:T(2,128)(2,1)S(1)}, u32[]{:S(2)}, u32[]{:S(2)}) async-start(bf16[4,2,14,14,256]{4,1,3,2,0:T(2,128)(2,1)} %copy.105), calls=%async_computation.2 | async-start | bytes 1605632 | tf_op jit(solution)/shard_map/all_to_all | solution.py:131
  121.6 1.5 copy-start.12
  121.6 163.3 %all-reduce.5.cloned.1.call-start = ((), (), s32[]{:S(2)}) async-start(), calls=%async_computation.3 | async-start | bytes 9437184 | tf_op jit(solution)/shard_map/psum | solution.py:136
  123.4 1.0 copy-start.13
  124.5 1.0 copy-start.5
  126.2 1.0 copy-start.11
  127.2 1.0 copy-start.7
  127.2 1.2 copy-start.9
  134.0 1.5 copy-start.2
  140.6 1.3 copy-start.15
  140.6 1.3 copy-start.16
  141.9 45.5 %copy-start.3 = (f32[16,8,5,256]{3,0,2,1:T(8,128)S(1)}, f32[16,8,5,256]{3,0,2,1:T(8,128)}, u32[]{:S(2)}) copy-start(f32[16,8,5,256]{3,0,2,1:T(8,128)} %copy.111) | copy-start | bytes 1966084
  187.6 2.6 collective-permute-start.4
  188.9 5.6 %collective-permute-start.5 = (bf16[1,32,256]{2,0,1:T(2,128)(2,1)S(1)}, bf16[1,32,256]{2,0,1:T(2,128)(2,1)S(1)}, u32[]{:S(2)}, u32[]{:S(2)}) collective-permute-start(bf16[1,32,256]{2,0,1:T(2,128)(2,1)S(1)} %get-tuple-element.172), channel_id=1, source_target_pairs={{4,0},{8,4},{12,8},{16,12},{20,16},{24,20},{28,24},{5,1},{9,5},{13... | collective-permute-start | bytes 49160 | tf_op jit(solution)/shard_map/ppermute | solution.py:18
  194.6 3.2 %collective-permute-start.6 = (bf16[18,1,256]{2,0,1:T(8,128)(2,1)S(1)}, bf16[18,1,256]{2,0,1:T(8,128)(2,1)S(1)}, u32[]{:S(2)}, u32[]{:S(2)}) collective-permute-start(bf16[18,1,256]{2,0,1:T(8,128)(2,1)S(1)} %get-tuple-element.167), channel_id=1, source_target_pairs={{0,1},{1,2},{2,3},{4,5},{5,6},{6,7},{8,9},{9,10},{10,11},{12,13},{... | collective-permute-start | bytes 27656 | tf_op jit(solution)/shard_map/ppermute | solution.py:17
  196.4 5.6 %collective-permute-start.7 = (bf16[18,1,256]{2,0,1:T(8,128)(2,1)S(1)}, bf16[18,1,256]{2,0,1:T(8,128)(2,1)S(1)}, u32[]{:S(2)}, u32[]{:S(2)}) collective-permute-start(bf16[18,1,256]{2,0,1:T(8,128)(2,1)S(1)} %get-tuple-element.168), channel_id=1, source_target_pairs={{1,0},{2,1},{3,2},{5,4},{6,5},{7,6},{9,8},{10,9},{11,10},{13,12},{... | collective-permute-start | bytes 27656 | tf_op jit(solution)/shard_map/ppermute | solution.py:18
  284.9 3.4 %copy-start.1 = (f32[3,3,256,256]{3,2,1,0:T(8,128)S(1)}, f32[3,3,256,256]{3,2,1,0:T(8,128)}, u32[]{:S(2)}) copy-start(f32[3,3,256,256]{3,2,1,0:T(8,128)} %get-tuple-element.154) | copy-start | bytes 7077892
Sparse Core Ops, SparseCore 0:
  138.8 146.0 all-reduce.4
where the time goes:
time: 298 us; the launch traced here: 297 us
  waiting for transfers between devices  123 us (41%)
  local copies, waits for them, and re-layouts  60.4 us (20%)
  loops' own time  31.5 us (11%)
  starting transfers between devices  27.2 us (9%)
  matrix products  27.2 us (9%)
  between operations  14.9 us (5%)
  other arithmetic  12.8 us (4%)
    psum x1, waiting for transfers between devices, body(): lax.psum((first_local, second_local), ('row', 'col'))  80.6 us
    another operation x1, loops' own time, body(): lax.fori_loop(0, slot_count, add_box, jnp.zeros((tile_rows, tile_cols, ch...  31.5 us
    all_to_all x1, waiting for transfers between devices, body(): lax.all_to_all(outgoing, 'col', split_axis=0, concat_axis=0, tiled=True)  22.7 us
    gather x24, local copies, waits for them, and re-layouts  19.9 us
    dot_general x18, matrix products, weight_grad(): lax.dot_general(window, flat_delta, (((0,), (0,)), ((), ())), preferred_e...  14 us
    ppermute x4, waiting for transfers between devices, padded_2(): after = lax.ppermute(leading, axis, down)  12.8 us
    ppermute x4, starting transfers between devices, padded_2(): before = lax.ppermute(last, axis, up)  11.1 us
    conv_general_dilated x7, matrix products, conv_pad(): lax.conv_general_dilated(inputs, kernel, (1, 1), ((margin, margin), (marg...  11.1 us
  transfers between devices with their start and end apart: 12, of which 9 were waited for; matrix products, arithmetic and copies ran while one was open for 13% of the time, Pallas kernels for 0%

commit v1 on v0

--- a/solution.py
+++ b/solution.py
@@ -5,6 +5,22 @@
 from jax.sharding import PartitionSpec as P
 
 LAYOUT = ("NHWC", "HWIO", "NHWC")
+
+
+def exchange_in_pairs(x, axis, split, join):
+    ways, here = (lax.axis_size(axis), lax.axis_index(axis))
+    width = x.shape[split] // ways
+    dims = list(x.shape)
+    dims[split] = width
+    height = dims[join]
+    dims[join] = height * ways
+    full = jnp.zeros(dims, x.dtype)
+    for mask in range(ways):
+        part = lax.dynamic_slice_in_dim(x, (here ^ mask) * width, width, axis=split)
+        if mask:
+            part = lax.ppermute(part, axis, [(d, d ^ mask) for d in range(ways)])
+        full = lax.dynamic_update_slice_in_dim(full, part, (here ^ mask) * height, axis=join)
+    return full
 
 
 def padded_2(shard, sides, width):
@@ -106,7 +122,7 @@
     )(top_row, left_col)
     outgoing = pick_rows(send_map, windows).reshape(columns, capacity, window, window, channels)
     arrived, arrived_head = (
-        lax.all_to_all(outgoing, "col", split_axis=0, concat_axis=0, tiled=True),
+        exchange_in_pairs(outgoing, "col", 0, 0),
         lax.all_to_all(pair_head, "col", split_axis=0, concat_axis=0, tiled=True),
     )
     arrived_head = arrived_head.reshape(pair_count, head_count)

time: 298 us -> 287 us (0.963)
  waiting for transfers between devices: 123 us -> 115 us
  local copies, waits for them, and re-layouts: 60.4 us -> 54.1 us
    all_to_all x1 -> x0, waiting for transfers between devices: 22.7 us -> none  [body(): lax.all_to_all(outgoing, 'col', split_axis=0, concat_axis=0, tiled=True)]
    ppermute x0 -> x3, waiting for transfers between devices: none -> 19.6 us  [exchange_in_pairs(): part = lax.ppermute(part, axis, [(d, d ^ mask) for d in range(ways)])]
    all_to_all x1, waiting for transfers between devices: 4.8 us -> 0.01 us  [body(): lax.all_to_all(pair_head, 'col', split_axis=0, concat_axis=0, tiled=True)]
    ppermute x0 -> x3, starting transfers between devices: none -> 4.45 us  [exchange_in_pairs(): part = lax.ppermute(part, axis, [(d, d ^ mask) for d in range(ways)])]
    gather x24, local copies, waits for them, and re-layouts: 19.9 us -> 15.6 us
    all_to_all x1 -> x0, starting transfers between devices: 3.99 us -> none  [body(): lax.all_to_all(outgoing, 'col', split_axis=0, concat_axis=0, tiled=True)]
    unnamed x49 -> x47, local copies, waits for them, and re-layouts: 9.91 us -> 7.71 us
  transfers between devices with their start and end apart: 12 -> 14, of which waited for: 9 -> 10; matrix products, arithmetic and copies ran while one was open for 13% -> 19% of each run, Pallas kernels for 0% -> 0%
where the time goes in v1:
time: 287 us; the launch traced here: 285 us
  waiting for transfers between devices  115 us (40%)
  local copies, waits for them, and re-layouts  54.1 us (19%)
  loops' own time  31.7 us (11%)
  starting transfers between devices  29.1 us (10%)
  matrix products  27 us (9%)
  between operations  14.9 us (5%)
  other arithmetic  13.5 us (5%)
    psum x1, waiting for transfers between devices, body(): lax.psum((first_local, second_local), ('row', 'col'))  79.8 us
    another operation x1, loops' own time, body(): lax.fori_loop(0, slot_count, add_box, jnp.zeros((tile_rows, tile_cols, ch...  31.5 us
    ppermute x3, waiting for transfers between devices, exchange_in_pairs(): part = lax.ppermute(part, axis, [(d, d ^ mask) for d in range(ways)])  19.6 us
    gather x24, local copies, waits for them, and re-layouts  15.6 us
    dot_general x18, matrix products, weight_grad(): lax.dot_general(window, flat_delta, (((0,), (0,)), ((), ())), preferred_e...  14 us
    ppermute x4, waiting for transfers between devices, padded_2(): after = lax.ppermute(leading, axis, down)  11.8 us
    conv_general_dilated x7, matrix products, conv_pad(): lax.conv_general_dilated(inputs, kernel, (1, 1), ((margin, margin), (marg...  11.1 us
    ppermute x4, starting transfers between devices, padded_2(): before = lax.ppermute(last, axis, up)  9.54 us
  transfers between devices with their start and end apart: 14, of which 10 were waited for; matrix products, arithmetic and copies ran while one was open for 19% of the time, Pallas kernels for 0%

profile of v1, /device:TPU:0, one launch (start us, length us, event | category | flops | bytes accessed | tf_op | source)
XLA Modules:
  0.0 285.5 jit_solution(9142593517253688962)
XLA Ops:
  11.7 6.3 %all-to-all-start = ((bf16[4,2,4]{2,1,0:T(2,128)(2,1)}), bf16[4,2,4]{2,1,0:T(2,128)(2,1)S(1)}, u32[]{:S(2)}, u32[]{:S(2)}) async-start(bf16[4,2,4]{2,1,0:T(2,128)(2,1)} %bitcast.9), calls=%async_computation | async-start | bytes 4096 | tf_op jit(solution)/shard_map/all_to_all | solution.py:126
  18.8 1.3 collective-permute-start.1
  20.1 3.0 %collective-permute-start = (bf16[1,32,256]{2,1,0:T(8,128)(2,1)S(1)}, bf16[1,32,256]{2,1,0:T(8,128)(2,1)S(1)}, u32[]{:S(2)}, u32[]{:S(2)}) collective-permute-start(bf16[1,32,256]{2,1,0:T(8,128)(2,1)S(1)} %get-tuple-element.178), channel_id=1, source_target_pairs={{0,4},{4,8},{8,12},{12,16},{16,20},{20,24},{24,28},{1,5},{5,9},{9,... | collective-permute-start | bytes 49160 | tf_op jit(solution)/shard_map/ppermute | solution.py:33
  25.0 3.9 %collective-permute-start.2 = (bf16[18,1,256]{2,1,0:T(2,128)(2,1)S(1)}, bf16[18,1,256]{2,1,0:T(2,128)(2,1)S(1)}, u32[]{:S(2)}, u32[]{:S(2)}) collective-permute-start(bf16[18,1,256]{2,1,0:T(2,128)(2,1)S(1)} %get-tuple-element.173), channel_id=1, source_target_pairs={{0,1},{1,2},{2,3},{4,5},{5,6},{6,7},{8,9},{9,10},{10,11},{12,13},{... | collective-permute-start | bytes 27656 | tf_op jit(solution)/shard_map/ppermute | solution.py:33
  28.9 1.3 collective-permute-start.3
  30.4 4.3 %collective-permute-done.3 = bf16[18,1,256]{2,1,0:T(2,128)(2,1)S(1)} collective-permute-done((bf16[18,1,256]{2,1,0:T(2,128)(2,1)S(1)}, bf16[18,1,256]{2,1,0:T(2,128)(2,1)S(1)}, u32[]{:S(2)}, u32[]{:S(2)}) %collective-permute-start.3) | collective-permute-done | bytes 9248 | tf_op jit(solution)/shard_map/ppermute | solution.py:34
  35.1 15.8 %while.15 = (s32[]{:T(128)}, bf16[18,34,256]{2,1,0:T(8,128)(2,1)S(1)}, s32[8,3]{0,1:T(4,128)S(1)}, bf16[8,16,16,256]{3,2,1,0:T(8,128)(2,1)S(1)}, s32[]{:T(128)}) while((s32[]{:T(128)}, bf16[18,34,256]{2,1,0:T(8,128)(2,1)S(1)}, s32[8,3]{0,1:T(4,128)S(1)}, bf16[8,16,16,256]{3,2,1,0:T(8,128)(2,1)S(1)}, s32[]{:T(128)}) %tuple.67), condition=%wide.while_cond, body=%wide.while_body.sunk | while | flops 2 | bytes 262269 | solution.py:121
  35.7 1.3 bitcast_dynamic-update-slice_fusion.2
  37.7 1.3 bitcast_dynamic-update-slice_fusion.2
  39.7 1.3 bitcast_dynamic-update-slice_fusion.2
  41.6 1.3 bitcast_dynamic-update-slice_fusion.2
  43.6 1.3 bitcast_dynamic-update-slice_fusion.2
  45.6 1.3 bitcast_dynamic-update-slice_fusion.2
  47.6 1.3 bitcast_dynamic-update-slice_fusion.2
  49.5 1.3 bitcast_dynamic-update-slice_fusion.2
  52.3 1.5 collective-permute-start.6
  53.8 1.5 collective-permute-start.5
  55.3 1.5 collective-permute-start.4
  57.7 1.1 copy.111
  58.8 12.1 %collective-permute-done.4 = bf16[1,2,16,16,256]{4,3,2,1,0:T(8,128)(2,1)S(1)} collective-permute-done((bf16[1,2,16,16,256]{4,3,2,1,0:T(8,128)(2,1)S(1)}, bf16[1,2,16,16,256]{4,3,2,1,0:T(8,128)(2,1)S(1)}, u32[]{:S(2)}, u32[]{:S(2)}) %collective-permute-start.4) | collective-permute-done | bytes 262176 | tf_op jit(solution)/shard_map/ppermute | solution.py:21
  70.9 7.4 %collective-permute-done.5 = bf16[1,2,16,16,256]{4,3,2,1,0:T(8,128)(2,1)S(1)} collective-permute-done((bf16[1,2,16,16,256]{4,3,2,1,0:T(8,128)(2,1)S(1)}, bf16[1,2,16,16,256]{4,3,2,1,0:T(8,128)(2,1)S(1)}, u32[]{:S(2)}, u32[]{:S(2)}) %collective-permute-start.5) | collective-permute-done | bytes 262176 | tf_op jit(solution)/shard_map/ppermute | solution.py:21
  80.1 1.3 multiply_convert_fusion.1
  82.6 1.2 fusion.43
  83.9 1.1 select_bitcast_fusion.1
  85.6 1.3 add_multiply_fusion
  88.3 1.2 fusion.62
  90.8 2.9 %fusion.9 = bf16[14,32,2,256]{3,1,2,0:T(8,128)(2,1)S(1)} fusion(bf16[3,3,256,256]{3,2,1,0:T(8,128)(2,1)} %param.13, bf16[14,4,7,2,256]{4,2,1,3,0:T(8,128)(2,1)S(1)} %slice.138, bf16[14,4,8,2,256]{4,2,1,3,0:T(8,128)(2,1)S(1)} %copy.102, f32[14,32,2,256]{3,1,2,0:T(8,128)} %copy-done.8, pred[32,2]{0,1:T(4,128)(4,1)S(1)} %copy-done.14), kind=kOutput, calls=%fused_computation.23 | convolution fusion | flops 1011679232 | bytes 3416128 | tf_op jit(solution)/shard_map/conv_general_dilated | solution.py:40
  95.3 2.4 copy.120
  97.8 1.2 reshape.164
  100.8 2.5 convolution_convert_fusion.4
  105.4 1.8 copy.105
  107.2 3.6 %all-to-all-start.1 = ((bf16[4,2,14,14,256]{4,1,3,2,0:T(2,128)(2,1)}), bf16[4,2,14,14,256]{4,1,3,2,0:T(2,128)(2,1)S(1)}, u32[]{:S(2)}, u32[]{:S(2)}) async-start(bf16[4,2,14,14,256]{4,1,3,2,0:T(2,128)(2,1)} %copy.105), calls=%async_computation.1 | async-start | bytes 1605632 | tf_op jit(solution)/shard_map/all_to_all | solution.py:147
  110.8 1.4 fusion.28
  119.6 1.1 fusion.17
  123.2 1.3 fusion.14
  124.6 1.1 fusion.13
  125.7 1.1 fusion.12
  127.8 3.6 %all-to-all-done.1 = bf16[4,2,14,14,256]{4,1,3,2,0:T(2,128)(2,1)S(1)} async-done(((bf16[4,2,14,14,256]{4,1,3,2,0:T(2,128)(2,1)}), bf16[4,2,14,14,256]{4,1,3,2,0:T(2,128)(2,1)S(1)}, u32[]{:S(2)}, u32[]{:S(2)}) %all-to-all-start.1) | async-done | bytes 802848 | tf_op jit(solution)/shard_map/all_to_all | solution.py:147
  132.9 45.5 %while.14 = (s32[]{:T(128)}, f32[16,32,256]{2,0,1:T(8,128)S(1)}, s32[8]{0:T(128)S(1)}, s32[8]{0:T(128)S(1)}, bf16[8,14,14,256]{3,2,1,0:T(8,128)(2,1)S(1)}, /*index=5*/s32[]{:T(128)}, s32[]{:T(128)}, s32[]{:T(128)}, s32[]{:T(128)}) while((s32[]{:T(128)}, f32[16,32,256]{2,0,1:T(8,128)S(1)}, s32[8]{0:T(128)S(1)}, s32[8]{0:T(128)S(1)}, ...), condition=%wide.region_2.3_spmd, body=%wide.region_1.2_spmd.sunk | while | flops 100360 | bytes 1706193 | solution.py:164
  178.7 1.3 collective-permute-start.7
  180.0 1.3 collective-permute-start.8
  181.3 3.1 %collective-permute-done.8 = bf16[1,32,256]{2,0,1:T(2,128)(2,1)S(1)} collective-permute-done((bf16[1,32,256]{2,0,1:T(2,128)(2,1)S(1)}, bf16[1,32,256]{2,0,1:T(2,128)(2,1)S(1)}, u32[]{:S(2)}, u32[]{:S(2)}) %collective-permute-start.8) | collective-permute-done | bytes 16416 | tf_op jit(solution)/shard_map/ppermute | solution.py:34
  184.4 1.3 collective-permute-start.9
  185.7 1.3 collective-permute-start.10
  187.1 4.4 %collective-permute-done.10 = bf16[18,1,256]{2,0,1:T(8,128)(2,1)S(1)} collective-permute-done((bf16[18,1,256]{2,0,1:T(8,128)(2,1)S(1)}, bf16[18,1,256]{2,0,1:T(8,128)(2,1)S(1)}, u32[]{:S(2)}, u32[]{:S(2)}) %collective-permute-start.10) | collective-permute-done | bytes 9248 | tf_op jit(solution)/shard_map/ppermute | solution.py:34
  193.8 79.8 %all-reduce.5.cloned.1.call-done = (f32[3,3,256,256]{3,2,1,0:T(8,128)}, f32[3,3,256,256]{3,2,1,0:T(8,128)}) async-done(((f32[3,3,256,256]{3,2,1,0:T(8,128)}, f32[3,3,256,256]{3,2,1,0:T(8,128)}), (f32[3,3,256,256]{3,2,1,0:T(8,128)}, f32[3,3,256,256]{3,2,1,0:T(8,128)})) %all-reduce.5.cloned.1.call-update) | async-done | bytes 4718608 | tf_op jit(solution)/shard_map/psum | solution.py:152
  273.6 3.4 %broadcast_multiply_fusion.1 = f32[3,3,256,256]{3,2,1,0:T(8,128)} fusion(f32[3,3,256,256]{3,2,1,0:T(8,128)} %get-tuple-element.153), kind=kLoop, calls=%fused_computation.29 | loop fusion | flops 589824 | bytes 4718592 | tf_op jit(solution)/shard_map/mul | solution.py:170
  277.0 1.6 broadcast_multiply_fusion
  (203 shorter events, 55.5 us)
Async XLA Ops:
  7.2 49.6 %copy-start = (bf16[3,3,256,256]{3,2,1,0:T(8,128)(2,1)S(1)}, bf16[3,3,256,256]{3,2,1,0:T(8,128)(2,1)}, u32[]{:S(2)}) copy-start(bf16[3,3,256,256]{3,2,1,0:T(8,128)(2,1)} %param.11) | copy-start | bytes 3538948
  11.7 67.2 %all-to-all-start = ((bf16[4,2,4]{2,1,0:T(2,128)(2,1)}), bf16[4,2,4]{2,1,0:T(2,128)(2,1)S(1)}, u32[]{:S(2)}, u32[]{:S(2)}) async-start(bf16[4,2,4]{2,1,0:T(2,128)(2,1)} %bitcast.9), calls=%async_computation | async-start | bytes 4096 | tf_op jit(solution)/shard_map/all_to_all | solution.py:126
  18.8 6.1 %collective-permute-start.1 = (bf16[1,32,256]{2,1,0:T(8,128)(2,1)S(1)}, bf16[1,32,256]{2,1,0:T(8,128)(2,1)S(1)}, u32[]{:S(2)}, u32[]{:S(2)}) collective-permute-start(bf16[1,32,256]{2,1,0:T(8,128)(2,1)S(1)} %get-tuple-element.177), channel_id=1, source_target_pairs={{4,0},{8,4},{12,8},{16,12},{20,16},{24,20},{28,24},{5,1},{9,5},{13... | collective-permute-start | bytes 49160 | tf_op jit(solution)/shard_map/ppermute | solution.py:34
  20.1 3.9 %collective-permute-start = (bf16[1,32,256]{2,1,0:T(8,128)(2,1)S(1)}, bf16[1,32,256]{2,1,0:T(8,128)(2,1)S(1)}, u32[]{:S(2)}, u32[]{:S(2)}) collective-permute-start(bf16[1,32,256]{2,1,0:T(8,128)(2,1)S(1)} %get-tuple-element.178), channel_id=1, source_target_pairs={{0,4},{4,8},{8,12},{12,16},{16,20},{20,24},{24,28},{1,5},{5,9},{9,... | collective-permute-start | bytes 49160 | tf_op jit(solution)/shard_map/ppermute | solution.py:33
  25.0 5.4 %collective-permute-start.2 = (bf16[18,1,256]{2,1,0:T(2,128)(2,1)S(1)}, bf16[18,1,256]{2,1,0:T(2,128)(2,1)S(1)}, u32[]{:S(2)}, u32[]{:S(2)}) collective-permute-start(bf16[18,1,256]{2,1,0:T(2,128)(2,1)S(1)} %get-tuple-element.173), channel_id=1, source_target_pairs={{0,1},{1,2},{2,3},{4,5},{5,6},{6,7},{8,9},{9,10},{10,11},{12,13},{... | collective-permute-start | bytes 27656 | tf_op jit(solution)/shard_map/ppermute | solution.py:33
  28.9 5.7 %collective-permute-start.3 = (bf16[18,1,256]{2,1,0:T(2,128)(2,1)S(1)}, bf16[18,1,256]{2,1,0:T(2,128)(2,1)S(1)}, u32[]{:S(2)}, u32[]{:S(2)}) collective-permute-start(bf16[18,1,256]{2,1,0:T(2,128)(2,1)S(1)} %get-tuple-element.174), channel_id=1, source_target_pairs={{1,0},{2,1},{3,2},{5,4},{6,5},{7,6},{9,8},{10,9},{11,10},{13,12},{... | collective-permute-start | bytes 27656 | tf_op jit(solution)/shard_map/ppermute | solution.py:34
  51.9 4.9 %copy-start.19 = (pred[8,5]{0,1:T(8,128)(4,1)S(1)}, pred[8,5]{0,1:T(8,128)(4,1)}, u32[]{:S(2)}) copy-start(pred[8,5]{0,1:T(8,128)(4,1)} %constant.137) | copy-start | bytes 124
  52.3 26.1 %collective-permute-start.6 = (bf16[1,2,16,16,256]{4,3,2,1,0:T(8,128)(2,1)S(1)}, bf16[1,2,16,16,256]{4,3,2,1,0:T(8,128)(2,1)S(1)}, u32[]{:S(2)}, u32[]{:S(2)}) collective-permute-start(bf16[1,2,16,16,256]{4,3,2,1,0:T(8,128)(2,1)S(1)} %get-tuple-element.159), channel_id=1, source_target_pairs={{0,3},{1,2},{2,1},{3,0},{4,7},{5,6},{6,5},{7,4},{8,11},{9,10},{10,... | collective-permute-start | bytes 786440 | tf_op jit(solution)/shard_map/ppermute | solution.py:21
  53.8 24.5 %collective-permute-start.5 = (bf16[1,2,16,16,256]{4,3,2,1,0:T(8,128)(2,1)S(1)}, bf16[1,2,16,16,256]{4,3,2,1,0:T(8,128)(2,1)S(1)}, u32[]{:S(2)}, u32[]{:S(2)}) collective-permute-start(bf16[1,2,16,16,256]{4,3,2,1,0:T(8,128)(2,1)S(1)} %get-tuple-element.160), channel_id=1, source_target_pairs={{0,2},{1,3},{2,0},{3,1},{4,6},{5,7},{6,4},{7,5},{8,10},{9,11},{10,... | collective-permute-start | bytes 786440 | tf_op jit(solution)/shard_map/ppermute | solution.py:21
  55.3 15.6 %collective-permute-start.4 = (bf16[1,2,16,16,256]{4,3,2,1,0:T(8,128)(2,1)S(1)}, bf16[1,2,16,16,256]{4,3,2,1,0:T(8,128)(2,1)S(1)}, u32[]{:S(2)}, u32[]{:S(2)}) collective-permute-start(bf16[1,2,16,16,256]{4,3,2,1,0:T(8,128)(2,1)S(1)} %get-tuple-element.161), channel_id=1, source_target_pairs={{0,1},{1,0},{2,3},{3,2},{4,5},{5,4},{6,7},{7,6},{8,9},{9,8},{10,11... | collective-permute-start | bytes 786440 | tf_op jit(solution)/shard_map/ppermute | solution.py:21
  79.4 0.7 copy-start.14
  81.3 1.3 copy-start.18
  83.8 1.2 copy-start.8
  83.8 1.8 copy-start.17
  89.4 0.8 copy-start.6
  94.4 6.3 %copy-start.4 = (bf16[14,4,16,256]{3,2,1,0:T(8,128)(2,1)}, bf16[14,4,16,256]{3,2,1,0:T(8,128)(2,1)S(1)}, u32[]{:S(2)}) copy-start(bf16[14,4,16,256]{3,2,1,0:T(8,128)(2,1)S(1)} %reshape.159) | copy-start | bytes 1376260
  105.4 5.4 %copy-start.10 = (bf16[4,14,14,256]{3,2,1,0:T(8,128)(2,1)S(1)}, bf16[4,14,14,256]{3,2,1,0:T(8,128)(2,1)}, u32[]{:S(2)}) copy-start(bf16[4,14,14,256]{3,2,1,0:T(8,128)(2,1)} %copy_bitcast_fusion.2) | copy-start | bytes 1204228
  107.2 24.3 %all-to-all-start.1 = ((bf16[4,2,14,14,256]{4,1,3,2,0:T(2,128)(2,1)}), bf16[4,2,14,14,256]{4,1,3,2,0:T(2,128)(2,1)S(1)}, u32[]{:S(2)}, u32[]{:S(2)}) async-start(bf16[4,2,14,14,256]{4,1,3,2,0:T(2,128)(2,1)} %copy.105), calls=%async_computation.1 | async-start | bytes 1605632 | tf_op jit(solution)/shard_map/all_to_all | solution.py:147
  110.8 1.4 copy-start.12
  110.8 162.8 %all-reduce.5.cloned.1.call-start = ((), (), s32[]{:S(2)}) async-start(), calls=%async_computation.2 | async-start | bytes 9437184 | tf_op jit(solution)/shard_map/psum | solution.py:152
  112.6 1.0 copy-start.13
  113.6 1.0 copy-start.5
  115.4 1.0 copy-start.11
  116.4 1.0 copy-start.7
  116.4 1.2 copy-start.9
  123.1 1.5 copy-start.2
  131.6 1.3 copy-start.15
  131.6 1.3 copy-start.16
  132.9 45.5 %copy-start.3 = (f32[16,8,5,256]{3,0,2,1:T(8,128)S(1)}, f32[16,8,5,256]{3,0,2,1:T(8,128)}, u32[]{:S(2)}) copy-start(f32[16,8,5,256]{3,0,2,1:T(8,128)} %copy.111) | copy-start | bytes 1966084
  178.7 2.6 collective-permute-start.7
  180.0 4.4 %collective-permute-start.8 = (bf16[1,32,256]{2,0,1:T(2,128)(2,1)S(1)}, bf16[1,32,256]{2,0,1:T(2,128)(2,1)S(1)}, u32[]{:S(2)}, u32[]{:S(2)}) collective-permute-start(bf16[1,32,256]{2,0,1:T(2,128)(2,1)S(1)} %get-tuple-element.176), channel_id=1, source_target_pairs={{4,0},{8,4},{12,8},{16,12},{20,16},{24,20},{28,24},{5,1},{9,5},{13... | collective-permute-start | bytes 49160 | tf_op jit(solution)/shard_map/ppermute | solution.py:34
  184.4 2.7 collective-permute-start.9
  185.7 5.8 %collective-permute-start.10 = (bf16[18,1,256]{2,0,1:T(8,128)(2,1)S(1)}, bf16[18,1,256]{2,0,1:T(8,128)(2,1)S(1)}, u32[]{:S(2)}, u32[]{:S(2)}) collective-permute-start(bf16[18,1,256]{2,0,1:T(8,128)(2,1)S(1)} %get-tuple-element.172), channel_id=1, source_target_pairs={{1,0},{2,1},{3,2},{5,4},{6,5},{7,6},{9,8},{10,9},{11,10},{13,12},{... | collective-permute-start | bytes 27656 | tf_op jit(solution)/shard_map/ppermute | solution.py:34
  273.6 3.4 %copy-start.1 = (f32[3,3,256,256]{3,2,1,0:T(8,128)S(1)}, f32[3,3,256,256]{3,2,1,0:T(8,128)}, u32[]{:S(2)}) copy-start(f32[3,3,256,256]{3,2,1,0:T(8,128)} %get-tuple-element.154) | copy-start | bytes 7077892
Sparse Core Ops, SparseCore 0:
  127.9 145.6 all-reduce.4
